TPU v7x, 32 devices: a whole 2x2x4 slice. The times are simulated.
32 devices in a mesh: seq: 8 (over z, core), tp: 4 (over y, x).
Axes of the slice: x: 2, y: 2, z: 4, core: 2. Of those that a mesh axis runs over, the one named last changes fastest.
Arguments:
- q_heads: bfloat16 [1024, 4096], P('seq', 'tp'), may hold values from -200 to 200
- k_heads: bfloat16 [1024, 4096], P('seq', 'tp'), may hold values from -4 to 4
- v_heads: bfloat16 [1024, 4096], P('seq', 'tp'), may hold values from -5 to 5
- grad_attn: bfloat16 [1024, 4096], P('seq', 'tp'), may hold values from -5 to 5
- attn_out: bfloat16 [1024, 4096], P('seq', 'tp'), may hold values from -5 to 5
- gate_q: bfloat16 [1024, 8192], P('seq', 'tp'), may hold values from -5 to 5
- feat_k: bfloat16 [1024, 8192], P('seq', 'tp'), may hold values from -5 to 5
- feat_v: bfloat16 [1024, 8192], P('seq', 'tp'), may hold values from -5 to 5
- conv_out: bfloat16 [1024, 8192], P('seq', 'tp'), may hold values from -5 to 5
- grad_y: bfloat16 [1024, 8192], P('seq', 'tp'), may hold values from -5 to 5
- filters: float32 [64, 128], replicated, may hold values from -0.5 to 0.5
Outputs:
- grad_q: bfloat16 [1024, 4096], P('seq', 'tp')
- grad_k: bfloat16 [1024, 4096], P('seq', 'tp')
- grad_v: bfloat16 [1024, 4096], P('seq', 'tp')
- grad_gate: bfloat16 [1024, 8192], P('seq', 'tp')
- grad_feat_k: bfloat16 [1024, 8192], P('seq', 'tp')
- grad_feat_v: bfloat16 [1024, 8192], P('seq', 'tp')
- grad_filters: float32 [64, 128], replicated
All inputs are finite; a program needn't handle non-finite values.
Results may differ from a plain program's by a relative error of at most 0.014.
Values may be sent and summed in bfloat16 or wider, within the bound.
A program may use at most 64 MiB of HBM per device.

v0:
```python
import functools

import jax
import jax.numpy as jnp
from jax import lax
from jax.experimental import pallas as pl
from jax.experimental.pallas import tpu as pltpu
from jax.sharding import PartitionSpec as P

HEADS = 32


def from_behind(value, axis, steps):
    count = lax.axis_size(axis)
    leading, last = (max(0, -steps), min(count, count - steps))
    return lax.ppermute(value, axis, [(source, source + steps) for source in range(leading, last)])


def wire_parts(x):
    high = x.astype(jnp.bfloat16)
    back = lax.optimization_barrier(high).astype(jnp.float32)
    low = (x - back).astype(jnp.bfloat16)
    return (high, low)


def local_ring(
    q_heads,
    k_heads,
    v_heads,
    grad_attn,
    attn_out,
    gate_q,
    feat_k,
    feat_v,
    conv_out,
    grad_y,
    filters,
):
    rows = q_heads.shape[0]
    heads_here = HEADS // lax.axis_size("tp")
    width = q_heads.shape[1] // heads_here
    scale = 1.0 / width**0.5
    shards = lax.axis_size("seq")
    place = lax.axis_index("seq")
    queries = q_heads.reshape(rows, heads_here, width)
    upstream = grad_attn.reshape(rows, heads_here, width)
    keys_here = k_heads.reshape(rows, heads_here, width)
    values_here = v_heads.reshape(rows, heads_here, width)
    delta = jnp.sum(
        upstream.astype(jnp.float32)
        * attn_out.reshape(rows, heads_here, width).astype(jnp.float32),
        axis=2,
    )
    delta_heads = delta.T
    diagonal = jnp.arange(rows)[:, None] >= jnp.arange(rows)[None, :]

    def query_tile(state, key_piece, value_piece, live):
        top, total, acc = state
        count = key_piece.shape[0]
        key_block = key_piece.reshape(count, heads_here, width)
        value_block = value_piece.reshape(count, heads_here, width)
        scores = (
            jnp.einsum("qhd,khd->hqk", queries, key_block, preferred_element_type=jnp.float32)
            * scale
        )
        top_new = jnp.maximum(top, jnp.max(jnp.where(live[None], scores, -1e30), axis=2))
        weights = jnp.where(live[None], jnp.exp(scores - top_new[:, :, None]), 0.0)
        decay = jnp.exp(top - top_new)
        dprob = jnp.einsum(
            "qhd,khd->hqk", upstream, value_block, preferred_element_type=jnp.float32
        )
        term = jnp.einsum(
            "hqk,khd->qhd",
            weights * (dprob - delta_heads[:, :, None]),
            key_block.astype(jnp.float32),
            precision=lax.Precision.HIGHEST,
        )
        return (top_new, total * decay + jnp.sum(weights, axis=2), acc * decay.T[:, :, None] + term)

    zero_rows = jnp.zeros((rows, heads_here, width), jnp.float32)
    state = (
        jnp.full((heads_here, rows), -1e30, jnp.float32),
        jnp.zeros((heads_here, rows), jnp.float32),
        zero_rows,
    )
    state = query_tile(state, k_heads, v_heads, diagonal)

    def relay_keys(back, carry):
        inner, moving = carry
        moving = from_behind((moving[0], moving[1]), "seq", 1)
        valid = place >= back
        live = jnp.broadcast_to(valid, (rows, rows))
        inner = query_tile(inner, moving[0], moving[1], live)
        return (inner, moving)

    state, moved = lax.fori_loop(1, shards, relay_keys, (state, (k_heads, v_heads)))
    top, total, acc = state
    lse = (top + jnp.log(total)).T
    grad_query = acc * (1.0 / total).T[:, :, None] * scale
    lse_high, lse_low = wire_parts(lse)
    delta_high, delta_low = wire_parts(delta)
    stats = jnp.stack([lse_high, lse_low, delta_high, delta_low], axis=1)

    def key_tile(inner, query_piece, upstream_piece, stat_piece, live):
        key_grad, value_grad = inner
        count = query_piece.shape[0]
        query_block = query_piece.reshape(count, heads_here, width)
        upstream_block = upstream_piece.reshape(count, heads_here, width)
        lse_w = stat_piece[:, 0].astype(jnp.float32) + stat_piece[:, 1].astype(jnp.float32)
        delta_w = stat_piece[:, 2].astype(jnp.float32) + stat_piece[:, 3].astype(jnp.float32)
        scores = (
            jnp.einsum("qhd,khd->hqk", query_block, keys_here, preferred_element_type=jnp.float32)
            * scale
        )
        probs = jnp.where(live[None], jnp.exp(scores - lse_w.T[:, :, None]), 0.0)
        dprob = jnp.einsum(
            "qhd,khd->hqk", upstream_block, values_here, preferred_element_type=jnp.float32
        )
        dscore = probs * (dprob - delta_w.T[:, :, None])
        value_grad = value_grad + jnp.einsum(
            "hqk,qhd->khd",
            probs.astype(jnp.bfloat16),
            upstream_block,
            preferred_element_type=jnp.float32,
        )
        key_grad = key_grad + jnp.einsum(
            "hqk,qhd->khd",
            dscore.astype(jnp.bfloat16),
            query_block,
            preferred_element_type=jnp.float32,
        )
        return (key_grad, value_grad)

    grads = (zero_rows, zero_rows)
    grads = key_tile(grads, q_heads, grad_attn, stats, diagonal)

    def relay_queries(back, carry):
        inner, moving = carry
        moving = from_behind((moving[0], moving[1], moving[2]), "seq", -1)
        valid = place + back <= shards - 1
        live = jnp.broadcast_to(valid, (rows, rows))
        inner = key_tile(inner, moving[0], moving[1], moving[2], live)
        return (inner, moving)

    grads, moved = lax.fori_loop(1, shards, relay_queries, (grads, (q_heads, grad_attn, stats)))
    key_grad, value_grad = grads
    grad_q = grad_query.astype(jnp.bfloat16).reshape(rows, heads_here * width)
    grad_k = (key_grad * scale).astype(jnp.bfloat16).reshape(rows, heads_here * width)
    grad_v = value_grad.astype(jnp.bfloat16).reshape(rows, heads_here * width)
    span_taps = filters.shape[1]
    groups = filters.shape[0]
    channels = gate_q.shape[1]
    dz = (grad_y.astype(jnp.float32) * gate_q.astype(jnp.float32)).astype(jnp.bfloat16)
    rim = from_behind(dz[: span_taps - 1], "seq", -1)
    grad_gate = (grad_y.astype(jnp.float32) * conv_out.astype(jnp.float32)).astype(jnp.bfloat16)
    padded = jnp.concatenate([dz, rim], axis=0).astype(jnp.float32)
    taps = jnp.tile(filters.T, (1, channels // groups))
    mixed = feat_k.astype(jnp.float32) * feat_v.astype(jnp.float32)
    numbers = ("NWC", "WIO", "NWC")
    dw = lax.conv_general_dilated(
        padded[None],
        taps[:, None, :],
        (1,),
        "VALID",
        dimension_numbers=numbers,
        feature_group_count=channels,
        precision=lax.Precision.HIGHEST,
    )[0]
    local_terms = lax.conv_general_dilated(
        padded[None],
        mixed[:, None, :],
        (1,),
        "VALID",
        dimension_numbers=numbers,
        feature_group_count=channels,
        precision=lax.Precision.HIGHEST,
    )[0]
    grad_feat_k = (dw * feat_v.astype(jnp.float32)).astype(jnp.bfloat16)
    grad_feat_v = (dw * feat_k.astype(jnp.float32)).astype(jnp.bfloat16)
    local_terms = jnp.sum(local_terms.reshape(span_taps, channels // groups, groups), axis=1).T
    filter_total = lax.psum(local_terms, ("seq", "tp"))
    count_all = rows * shards * channels * lax.axis_size("tp") / groups
    grad_filters = filter_total * (1.0 / count_all**0.5)
    return (grad_q, grad_k, grad_v, grad_gate, grad_feat_k, grad_feat_v, grad_filters)


MESH = pl.DeviceIdType.MESH
LANES = 128
LOG2E = 1.4426950408889634


def kernel(
    n,
    tp,
    q_in,
    k_in,
    v_in,
    do_in,
    ao_in,
    gate_in,
    fk_in,
    fv_in,
    co_in,
    gy_in,
    filters,
    gq_out,
    gk_out,
    gv_out,
    gg_out,
    gfk_out,
    gfv_out,
    gf_out,
    heads_q,
    heads_k,
    heads_v,
    heads_do,
    keys_t,
    delta_mine,
    delta_all,
    do_here,
    ao_here,
    gate,
    fk,
    fv,
    co,
    gy,
    dz_here,
    dz_rim,
    dz_all,
    rim_all,
    dw_all,
    taps,
    terms,
    partial_mine,
    partial_in,
    across,
    scores,
    acc_k,
    acc_v,
    res_q,
    res_k,
    res_v,
    load_sem,
    own_sem,
    send_in,
    recv_in,
    send_rim,
    recv_rim,
    send_out,
    recv_out,
    own_out,
    send_rs,
    recv_rs,
    send_tp,
    recv_tp,
    send_ag,
    recv_ag,
):
    me = lax.axis_index("seq")
    lane = lax.axis_index("tp")
    rows, width = q_in.shape[0], q_in.shape[1] // n
    channels = gy_in.shape[1]
    span = filters.shape[1]
    scale = 1.0 / width**0.5

    loads = [
        pltpu.make_async_copy(src, dst, load_sem.at[i])
        for i, (src, dst) in enumerate(
            (
                (gy_in, gy),
                (gate_in, gate),
                (do_in, do_here),
                (ao_in, ao_here),
                (fk_in, fk),
                (fv_in, fv),
                (co_in, co),
            )
        )
    ]
    for load in loads:
        load.start()

    barrier = pltpu.get_barrier_semaphore()
    for d in range(1, n):
        pl.semaphore_signal(
            barrier, inc=1, device_id={"seq": lax.rem(me + d, n)}, device_id_type=MESH
        )
    for d in range(1, tp):
        pl.semaphore_signal(
            barrier, inc=1, device_id={"tp": lax.rem(lane + d, tp)}, device_id_type=MESH
        )
    pl.semaphore_wait(barrier, n - 1 + tp - 1)

    def cols(i):
        return pl.ds(pl.multiple_of(i * width, width), width)

    def block(i):
        return pl.ds(pl.multiple_of(i * rows, rows), rows)

    arrays = ((q_in, heads_q), (k_in, heads_k), (v_in, heads_v), (do_in, heads_do))
    sends = []
    for a, (src, dst) in enumerate(arrays):
        own = pltpu.make_async_copy(src.at[:, cols(me)], dst.at[block(me), :], own_sem.at[a])
        own.start()
        sends.append((0, own))
        for d in range(1, n):
            peer = lax.rem(me + d, n)
            copy = pltpu.make_async_remote_copy(
                src_ref=src.at[:, cols(peer)],
                dst_ref=dst.at[block(me), :],
                send_sem=send_in.at[a, d],
                recv_sem=recv_in.at[a, d],
                device_id={"seq": peer},
                device_id_type=MESH,
            )
            sends.append((d, copy))

    loads[0].wait()
    loads[1].wait()
    tiles = channels // LANES
    for t in range(tiles):
        at = slice(t * LANES, (t + 1) * LANES)
        dz = (gy[:, at].astype(jnp.float32) * gate[:, at].astype(jnp.float32)).astype(jnp.bfloat16)
        dz_here[:, at] = dz
        dz_all[t, 0:rows, :] = dz.astype(jnp.float32)
        dz_all[t, rows : rows + 8, :] = jnp.zeros((8, LANES), jnp.float32)

    def rim_copy():
        return pltpu.make_async_remote_copy(
            src_ref=dz_here,
            dst_ref=dz_rim,
            send_sem=send_rim,
            recv_sem=recv_rim,
            device_id={"seq": lax.rem(me + n - 1, n)},
            device_id_type=MESH,
        )

    @pl.when(me > 0)
    def _():
        rim_copy().start()

    for d, copy in sends:
        if d > 0:
            copy.start()


    loads[2].wait()
    loads[3].wait()
    for h in range(n):
        at = slice(h * width, (h + 1) * width)
        prod = do_here[:, at].astype(jnp.float32) * ao_here[:, at].astype(jnp.float32)
        line = jnp.sum(prod.T, axis=0, keepdims=True)
        delta_mine[h] = jnp.broadcast_to(line, (8, rows))
    delta_all[me] = delta_mine[me]
    deltas = []
    for d in range(1, n):
        peer = lax.rem(me + d, n)
        copy = pltpu.make_async_remote_copy(
            src_ref=delta_mine.at[peer],
            dst_ref=delta_all.at[me],
            send_sem=send_in.at[4, d],
            recv_sem=recv_in.at[4, d],
            device_id={"seq": peer},
            device_id_type=MESH,
        )
        copy.start()
        deltas.append(copy)

    loads[4].wait()
    loads[5].wait()
    loads[6].wait()
    for t in range(tiles):
        at = slice(t * LANES, (t + 1) * LANES)
        gg_out[:, at] = (gy[:, at].astype(jnp.float32) * co[:, at].astype(jnp.float32)).astype(
            jnp.bfloat16
        )
    terms[...] = jnp.zeros_like(terms)
    both = jnp.concatenate([filters[...]] * (LANES // filters.shape[0]), axis=0)
    taps[...] = both.T

    def conv_own(t, carry):
        at = pl.ds(pl.multiple_of(t * LANES, LANES), LANES)
        mixed = fk[:, at].astype(jnp.float32) * fv[:, at].astype(jnp.float32)
        for a in range(span // 8):
            size = rows - 8 * a
            part = None
            for b in range(8):
                tap = 8 * a + b
                x = dz_all[t, tap : tap + size, :]
                term = x * taps[tap : tap + 1, :]
                part = term if part is None else part + term
                prod = (x * mixed[0:size]).reshape(size // 8, 8, LANES)
                terms[tap] = terms[tap] + jnp.sum(prod, axis=0)
            if a == 0:
                dw_all[t] = part
            else:
                dw_all[t, 0:size, :] = dw_all[t, 0:size, :] + part
        return carry

    lax.fori_loop(0, tiles, conv_own, 0)

    for d, copy in sends:
        if d == 0:
            copy.wait()
        else:
            copy.wait_recv()
    for copy in deltas:
        copy.wait_recv()
    tile = 2 * rows
    steps = n * rows // tile
    for j in range(steps):
        at = slice(j * tile, (j + 1) * tile)
        keys_t[:, at] = heads_k[at, :].T
    acc_k[...] = jnp.zeros_like(acc_k)
    acc_v[...] = jnp.zeros_like(acc_v)
    key_id = lax.broadcasted_iota(jnp.int32, (tile, tile), 0)
    query_id = lax.broadcasted_iota(jnp.int32, (tile, tile), 1)
    nt = (((1,), (1,)), ((), ()))
    nn = (((1,), (0,)), ((), ()))

    def dot(a, b, dims):
        return lax.dot_general(a, b, dims, preferred_element_type=jnp.float32)

    results = ((res_q, gq_out), (res_k, gk_out), (res_v, gv_out))

    def out_copy(a, r, src_rows):
        src, dst = results[a]
        return pltpu.make_async_remote_copy(
            src_ref=src.at[src_rows, :],
            dst_ref=dst.at[:, cols(me)],
            send_sem=send_out.at[a, r],
            recv_sem=recv_out.at[a, me],
            device_id={"seq": r},
            device_id_type=MESH,
        )

    def own_copy(a, r):
        src, dst = results[a]
        return pltpu.make_async_copy(src.at[block(r), :], dst.at[:, cols(me)], own_out.at[a])

    for i in reversed(range(steps)):
        at_q = slice(i * tile, (i + 1) * tile)
        query = heads_q[at_q, :]
        upstream = heads_do[at_q, :]
        delta = jnp.concatenate(
            [delta_all[2 * i][0:1, :], delta_all[2 * i + 1][0:1, :]], axis=1
        )
        top = None
        for j in range(i + 1):
            at_k = slice(j * tile, (j + 1) * tile)
            raw = dot(heads_k[at_k, :], query, nt)
            if j == i:
                raw = jnp.where(key_id <= query_id, raw, -1e30)
            scores[at_k, :] = raw
            high = jnp.max(raw, axis=0, keepdims=True)
            top = high if top is None else jnp.maximum(top, high)
        total = jnp.zeros_like(top)
        for j in range(i + 1):
            at_k = slice(j * tile, (j + 1) * tile)
            weight = jnp.exp2((scores[at_k, :] - top) * (scale * LOG2E))
            scores[at_k, :] = weight
            total = total + jnp.sum(weight, axis=0, keepdims=True)
        lse = top * scale + jnp.log(total)
        lse_high = lse.astype(jnp.bfloat16).astype(jnp.float32)
        lse_w = lse_high + (lse - lse_high).astype(jnp.bfloat16).astype(jnp.float32)
        delta_high = delta.astype(jnp.bfloat16).astype(jnp.float32)
        delta_w = delta_high + (delta - delta_high).astype(jnp.bfloat16).astype(jnp.float32)
        share_q = 1.0 / total
        share_k = share_q * jnp.exp(lse - lse_w)
        grad_t = jnp.zeros((width, tile), jnp.float32)
        for j in range(i + 1):
            at_k = slice(j * tile, (j + 1) * tile)
            weight = scores[at_k, :]
            dprob = dot(heads_v[at_k, :], upstream, nt)
            dscore = (weight * share_q) * (dprob - delta)
            probs_k = weight * share_k
            dscore_k = (probs_k * (dprob - delta_w)).astype(jnp.bfloat16)
            big = dscore.astype(jnp.bfloat16)
            rest = (dscore - big.astype(jnp.float32)).astype(jnp.bfloat16)
            grad_t = grad_t + dot(keys_t[:, at_k], big, nn) + dot(keys_t[:, at_k], rest, nn)
            acc_v[at_k, :] = acc_v[at_k, :] + dot(probs_k.astype(jnp.bfloat16), upstream, nn)
            acc_k[at_k, :] = acc_k[at_k, :] + dot(dscore_k, query, nn)
        res_q[at_q, :] = (grad_t * scale).T.astype(jnp.bfloat16)
        res_k[at_q, :] = (acc_k[at_q, :] * scale).astype(jnp.bfloat16)
        res_v[at_q, :] = acc_v[at_q, :].astype(jnp.bfloat16)
        for r in (2 * i, 2 * i + 1):

            @pl.when(me != r)
            def _():
                for a in range(3):
                    out_copy(a, r, slice(r * rows, (r + 1) * rows)).start()

            @pl.when(me == r)
            def _():
                for a in range(3):
                    own_copy(a, r).start()

    @pl.when(me < n - 1)
    def _():
        rim_copy().wait_recv()
        for t in range(tiles):
            at = slice(t * LANES, (t + 1) * LANES)
            rim_all[t, 0:8, :] = jnp.zeros((8, LANES), jnp.float32)
            rim_all[t, 8 : rows + 8, :] = dz_rim[:, at].astype(jnp.float32)

    @pl.when(me == n - 1)
    def _():
        for t in range(tiles):
            rim_all[t, 0 : rows + 8, :] = jnp.zeros((rows + 8, LANES), jnp.float32)

    def conv_rim(t, carry):
        at = pl.ds(pl.multiple_of(t * LANES, LANES), LANES)
        left = fk[:, at].astype(jnp.float32)
        right = fv[:, at].astype(jnp.float32)
        mixed = left * right
        for a in range(span // 8):
            size = 8 * (a + 1)
            part = None
            for b in range(8):
                tap = 8 * a + b
                x = rim_all[t, b : b + size, :]
                term = x * taps[tap : tap + 1, :]
                part = term if part is None else part + term
                prod = (x * mixed[rows - size : rows]).reshape(size // 8, 8, LANES)
                terms[tap] = terms[tap] + jnp.sum(prod, axis=0)
            dw_all[t, rows - size : rows, :] = dw_all[t, rows - size : rows, :] + part
        acc = dw_all[t]
        gfk_out[:, at] = (acc * right).astype(jnp.bfloat16)
        gfv_out[:, at] = (acc * left).astype(jnp.bfloat16)
        return carry

    lax.fori_loop(0, tiles, conv_rim, 0)
    per_lane = jnp.sum(terms[...], axis=1)
    groups = gf_out.shape[0]
    folded = per_lane
    for g in range(1, LANES // groups):
        folded = folded + pltpu.roll(per_lane, g * groups, 1)
    share = groups // n
    partial_mine[...] = folded.T[0:groups, :]

    def slab(i):
        return pl.ds(pl.multiple_of(i * share, share), share)

    partial_in[me] = partial_mine[slab(me), :]
    small = []
    for d in range(1, n):
        peer = lax.rem(me + d, n)
        copy = pltpu.make_async_remote_copy(
            src_ref=partial_mine.at[slab(peer), :],
            dst_ref=partial_in.at[me],
            send_sem=send_rs.at[d],
            recv_sem=recv_rs.at[d],
            device_id={"seq": peer},
            device_id_type=MESH,
        )
        copy.start()
        small.append(copy)

    for copy in small:
        copy.wait_recv()
    total = partial_in[0]
    for i in range(1, n):
        total = total + partial_in[i]
    across[lane] = total
    crossing = []
    for d in range(1, tp):
        copy = pltpu.make_async_remote_copy(
            src_ref=across.at[lane],
            dst_ref=across.at[lane],
            send_sem=send_tp.at[d],
            recv_sem=recv_tp.at[d],
            device_id={"tp": lax.rem(lane + d, tp)},
            device_id_type=MESH,
        )
        copy.start()
        crossing.append(copy)

    for copy in crossing:
        copy.wait_recv()
    total = across[0]
    for i in range(1, tp):
        total = total + across[i]
    count_all = rows * n * channels * tp / groups
    gf_out[slab(me), :] = total * (1.0 / count_all**0.5)
    gather = []
    for d in range(1, n):
        copy = pltpu.make_async_remote_copy(
            src_ref=gf_out.at[slab(me), :],
            dst_ref=gf_out.at[slab(me), :],
            send_sem=send_ag.at[d],
            recv_sem=recv_ag.at[d],
            device_id={"seq": lax.rem(me + d, n)},
            device_id_type=MESH,
        )
        copy.start()
        gather.append(copy)

    @pl.when(me > 0)
    def _():
        rim_copy().wait_send()

    for d, copy in sends:
        if d > 0:
            copy.wait_send()
    for copy in deltas + small + crossing:
        copy.wait_send()

    for r in range(n):

        @pl.when(me != r)
        def _():
            for a in range(3):
                out_copy(a, r, slice(r * rows, (r + 1) * rows)).wait_send()

    for a in range(3):
        own_copy(a, me).wait()
        for d in range(1, n):
            peer = lax.rem(me + d, n)
            src, dst = results[a]
            pltpu.make_async_remote_copy(
                src_ref=src.at[block(me), :],
                dst_ref=dst.at[:, cols(peer)],
                send_sem=send_out.at[a, peer],
                recv_sem=recv_out.at[a, peer],
                device_id={"seq": peer},
                device_id_type=MESH,
            ).wait_recv()
    for copy in gather:
        copy.wait()


def local_heads(
    n,
    tp,
    q_heads,
    k_heads,
    v_heads,
    grad_attn,
    attn_out,
    gate_q,
    feat_k,
    feat_v,
    conv_out,
    grad_y,
    filters,
):
    rows, wide = q_heads.shape
    width = wide // n
    channels = gate_q.shape[1]
    groups, span = filters.shape
    share = groups // n
    tiles = channels // LANES
    bf16, f32 = (jnp.bfloat16, jnp.float32)
    anywhere = pl.BlockSpec(memory_space=pl.ANY)
    inside = pl.BlockSpec(memory_space=pltpu.VMEM)
    dma = pltpu.SemaphoreType.DMA
    return pl.pallas_call(
        functools.partial(kernel, n, tp),
        out_shape=(
            [jax.ShapeDtypeStruct((rows, wide), bf16)] * 3
            + [jax.ShapeDtypeStruct((rows, channels), bf16)] * 3
            + [jax.ShapeDtypeStruct((groups, span), f32)]
        ),
        in_specs=[anywhere] * 10 + [inside],
        out_specs=[anywhere] * 3 + [inside] * 4,
        scratch_shapes=(
            [pltpu.VMEM((n * rows, width), bf16)] * 4
            + [
                pltpu.VMEM((width, n * rows), bf16),
                pltpu.VMEM((n, 8, rows), f32),
                pltpu.VMEM((n, 8, rows), f32),
            ]
            + [pltpu.VMEM((rows, wide), bf16)] * 2
            + [pltpu.VMEM((rows, channels), bf16)] * 7
            + [
                pltpu.VMEM((tiles, rows + 8, LANES), f32),
                pltpu.VMEM((tiles, rows + 16, LANES), f32),
                pltpu.VMEM((tiles, rows, LANES), f32),
                pltpu.VMEM((span, LANES), f32),
                pltpu.VMEM((span, 8, LANES), f32),
                pltpu.VMEM((groups, span), f32),
                pltpu.VMEM((n, share, span), f32),
                pltpu.VMEM((tp, share, span), f32),
                pltpu.VMEM((n * rows, 2 * rows), f32),
            ]
            + [pltpu.VMEM((n * rows, width), f32)] * 2
            + [pltpu.VMEM((n * rows, width), bf16)] * 3
            + [
                dma((7,)),
                dma((4,)),
                dma((5, n)),
                dma((5, n)),
                dma,
                dma,
                dma((3, n)),
                dma((3, n)),
                dma((3,)),
                dma((n,)),
                dma((n,)),
                dma((tp,)),
                dma((tp,)),
                dma((n,)),
                dma((n,)),
            ]
        ),
        compiler_params=pltpu.CompilerParams(
            collective_id=0, has_side_effects=True, vmem_limit_bytes=67043328
        ),
    )(
        q_heads,
        k_heads,
        v_heads,
        grad_attn,
        attn_out,
        gate_q,
        feat_k,
        feat_v,
        conv_out,
        grad_y,
        filters,
    )


def local(*args):
    n, tp = (lax.axis_size("seq"), lax.axis_size("tp"))
    rows, wide = args[0].shape
    groups, span = args[10].shape
    fits = (
        HEADS // tp == n
        and n > 1
        and tp > 1
        and n % 2 == 0
        and rows == LANES
        and wide == n * LANES
        and span <= rows
        and span == LANES
        and LANES % groups == 0
        and groups % (8 * n) == 0
    )
    if fits:
        return tuple(local_heads(n, tp, *args))
    return local_ring(*args)


def solution(mesh):
    in_specs = (
        P("seq", "tp"),
        P("seq", "tp"),
        P("seq", "tp"),
        P("seq", "tp"),
        P("seq", "tp"),
        P("seq", "tp"),
        P("seq", "tp"),
        P("seq", "tp"),
        P("seq", "tp"),
        P("seq", "tp"),
        P(),
    )
    out_specs = (
        P("seq", "tp"),
        P("seq", "tp"),
        P("seq", "tp"),
        P("seq", "tp"),
        P("seq", "tp"),
        P("seq", "tp"),
        P(),
    )
    return jax.shard_map(local, mesh=mesh, in_specs=in_specs, out_specs=out_specs, check_vma=False)
```

profile of v0, /device:TPU:0, one launch (start us, length us, event | category | flops | bytes accessed | tf_op | source)
XLA Modules:
  0.0 75.5 jit_solution(3623835041273161515)
XLA Ops:
  0.6 67.8 %shard_map.162 = (bf16[128,1024]{1,0:T(8,128)(2,1)}, bf16[128,1024]{1,0:T(8,128)(2,1)}, bf16[128,1024]{1,0:T(8,128)(2,1)}, bf16[128,2048]{1,0:T(8,128)(2,1)}, bf...) custom-call(bf16[128,1024]{1,0:T(8,128)(2,1)} %q_in.1, bf16[128,1024]{1,0:T(8,128)(2,1)} %k_in.1, ...), custom_call_target="tpu_custom_call" | custom-call | tf_op jit(solution)/shard_map/pallas_call | solution.py:657
  68.5 0.0 copy-start.4
  68.5 0.0 copy-start.3
  68.5 1.7 %copy.25 = bf16[128,1024]{1,0:T(8,128)(2,1)} copy(bf16[128,1024]{1,0:T(8,128)(2,1)} %get-tuple-element.14) | data formatting | bytes 524288
  70.2 0.0 copy-done.4
  70.2 0.0 copy-start.2
  70.2 0.7 copy.26
  70.9 0.0 copy-done.3
  70.9 0.7 copy.27
  71.6 0.0 copy-done.2
  71.6 0.0 copy-start.1
  71.6 0.8 %copy.28 = bf16[128,2048]{1,0:T(8,128)(2,1)} copy(bf16[128,2048]{1,0:T(8,128)(2,1)S(1)} %copy-done.2) | data formatting | bytes 1048576
  72.4 0.4 copy-done.1
  72.9 0.0 copy-start
  72.9 0.8 %copy.29 = bf16[128,2048]{1,0:T(8,128)(2,1)} copy(bf16[128,2048]{1,0:T(8,128)(2,1)S(1)} %copy-done.1) | data formatting | bytes 1048576
  73.7 0.4 copy-done
  74.1 0.0 copy-start.5
  74.1 0.8 %copy.30 = bf16[128,2048]{1,0:T(8,128)(2,1)} copy(bf16[128,2048]{1,0:T(8,128)(2,1)S(1)} %copy-done) | data formatting | bytes 1048576
  74.9 0.0 copy-done.5
  74.9 0.6 copy.31
Async XLA Ops:
  68.5 1.7 %copy-start.4 = (bf16[128,1024]{1,0:T(8,128)(2,1)S(1)}, bf16[128,1024]{1,0:T(8,128)(2,1)}, u32[]{:S(2)}) copy-start(bf16[128,1024]{1,0:T(8,128)(2,1)} %get-tuple-element.15) | copy-start | bytes 786436
  68.5 2.4 %copy-start.3 = (bf16[128,1024]{1,0:T(8,128)(2,1)S(1)}, bf16[128,1024]{1,0:T(8,128)(2,1)}, u32[]{:S(2)}) copy-start(bf16[128,1024]{1,0:T(8,128)(2,1)} %get-tuple-element.16) | copy-start | bytes 786436
  70.2 1.4 %copy-start.2 = (bf16[128,2048]{1,0:T(8,128)(2,1)S(1)}, bf16[128,2048]{1,0:T(8,128)(2,1)}, u32[]{:S(2)}) copy-start(bf16[128,2048]{1,0:T(8,128)(2,1)} %get-tuple-element.17) | copy-start | bytes 1572868
  71.6 1.2 %copy-start.1 = (bf16[128,2048]{1,0:T(8,128)(2,1)S(1)}, bf16[128,2048]{1,0:T(8,128)(2,1)}, u32[]{:S(2)}) copy-start(bf16[128,2048]{1,0:T(8,128)(2,1)} %get-tuple-element.18) | copy-start | bytes 1572868
  72.9 1.2 %copy-start = (bf16[128,2048]{1,0:T(8,128)(2,1)S(1)}, bf16[128,2048]{1,0:T(8,128)(2,1)}, u32[]{:S(2)}) copy-start(bf16[128,2048]{1,0:T(8,128)(2,1)} %get-tuple-element.19) | copy-start | bytes 1572868
  74.1 0.8 %copy-start.5 = (f32[64,128]{1,0:T(8,128)S(1)}, f32[64,128]{1,0:T(8,128)}, u32[]{:S(2)}) copy-start(f32[64,128]{1,0:T(8,128)} %get-tuple-element.20) | copy-start | bytes 98308
where the time goes:
time: 75.8 us; the launch traced here: 75.5 us
  Pallas kernels  67.8 us (89%)
  local copies, waits for them, and re-layouts  7.01 us (9%)
    pallas_call x1, Pallas kernels, local_heads(): pl.pallas_call(functools.partial(kernel, n, tp), out_shape=[jax.ShapeDtyp...  67.8 us
    unnamed x19, local copies, waits for them, and re-layouts  7.01 us

commit v1 on v0

v1 whole, which is shorter than its diff:
```python
import functools

import jax
import jax.numpy as jnp
from jax import lax
from jax.experimental import pallas as pl
from jax.experimental.pallas import tpu as pltpu
from jax.sharding import PartitionSpec as P

HEADS = 32


def from_behind(value, axis, steps):
    count = lax.axis_size(axis)
    leading, last = (max(0, -steps), min(count, count - steps))
    return lax.ppermute(value, axis, [(source, source + steps) for source in range(leading, last)])


def wire_parts(x):
    high = x.astype(jnp.bfloat16)
    back = lax.optimization_barrier(high).astype(jnp.float32)
    low = (x - back).astype(jnp.bfloat16)
    return (high, low)


def local_ring(
    q_heads,
    k_heads,
    v_heads,
    grad_attn,
    attn_out,
    gate_q,
    feat_k,
    feat_v,
    conv_out,
    grad_y,
    filters,
):
    rows = q_heads.shape[0]
    heads_here = HEADS // lax.axis_size("tp")
    width = q_heads.shape[1] // heads_here
    scale = 1.0 / width**0.5
    shards = lax.axis_size("seq")
    place = lax.axis_index("seq")
    queries = q_heads.reshape(rows, heads_here, width)
    upstream = grad_attn.reshape(rows, heads_here, width)
    keys_here = k_heads.reshape(rows, heads_here, width)
    values_here = v_heads.reshape(rows, heads_here, width)
    delta = jnp.sum(
        upstream.astype(jnp.float32)
        * attn_out.reshape(rows, heads_here, width).astype(jnp.float32),
        axis=2,
    )
    delta_heads = delta.T
    diagonal = jnp.arange(rows)[:, None] >= jnp.arange(rows)[None, :]

    def query_tile(state, key_piece, value_piece, live):
        top, total, acc = state
        count = key_piece.shape[0]
        key_block = key_piece.reshape(count, heads_here, width)
        value_block = value_piece.reshape(count, heads_here, width)
        scores = (
            jnp.einsum("qhd,khd->hqk", queries, key_block, preferred_element_type=jnp.float32)
            * scale
        )
        top_new = jnp.maximum(top, jnp.max(jnp.where(live[None], scores, -1e30), axis=2))
        weights = jnp.where(live[None], jnp.exp(scores - top_new[:, :, None]), 0.0)
        decay = jnp.exp(top - top_new)
        dprob = jnp.einsum(
            "qhd,khd->hqk", upstream, value_block, preferred_element_type=jnp.float32
        )
        term = jnp.einsum(
            "hqk,khd->qhd",
            weights * (dprob - delta_heads[:, :, None]),
            key_block.astype(jnp.float32),
            precision=lax.Precision.HIGHEST,
        )
        return (top_new, total * decay + jnp.sum(weights, axis=2), acc * decay.T[:, :, None] + term)

    zero_rows = jnp.zeros((rows, heads_here, width), jnp.float32)
    state = (
        jnp.full((heads_here, rows), -1e30, jnp.float32),
        jnp.zeros((heads_here, rows), jnp.float32),
        zero_rows,
    )
    state = query_tile(state, k_heads, v_heads, diagonal)

    def relay_keys(back, carry):
        inner, moving = carry
        moving = from_behind((moving[0], moving[1]), "seq", 1)
        valid = place >= back
        live = jnp.broadcast_to(valid, (rows, rows))
        inner = query_tile(inner, moving[0], moving[1], live)
        return (inner, moving)

    state, moved = lax.fori_loop(1, shards, relay_keys, (state, (k_heads, v_heads)))
    top, total, acc = state
    lse = (top + jnp.log(total)).T
    grad_query = acc * (1.0 / total).T[:, :, None] * scale
    lse_high, lse_low = wire_parts(lse)
    delta_high, delta_low = wire_parts(delta)
    stats = jnp.stack([lse_high, lse_low, delta_high, delta_low], axis=1)

    def key_tile(inner, query_piece, upstream_piece, stat_piece, live):
        key_grad, value_grad = inner
        count = query_piece.shape[0]
        query_block = query_piece.reshape(count, heads_here, width)
        upstream_block = upstream_piece.reshape(count, heads_here, width)
        lse_w = stat_piece[:, 0].astype(jnp.float32) + stat_piece[:, 1].astype(jnp.float32)
        delta_w = stat_piece[:, 2].astype(jnp.float32) + stat_piece[:, 3].astype(jnp.float32)
        scores = (
            jnp.einsum("qhd,khd->hqk", query_block, keys_here, preferred_element_type=jnp.float32)
            * scale
        )
        probs = jnp.where(live[None], jnp.exp(scores - lse_w.T[:, :, None]), 0.0)
        dprob = jnp.einsum(
            "qhd,khd->hqk", upstream_block, values_here, preferred_element_type=jnp.float32
        )
        dscore = probs * (dprob - delta_w.T[:, :, None])
        value_grad = value_grad + jnp.einsum(
            "hqk,qhd->khd",
            probs.astype(jnp.bfloat16),
            upstream_block,
            preferred_element_type=jnp.float32,
        )
        key_grad = key_grad + jnp.einsum(
            "hqk,qhd->khd",
            dscore.astype(jnp.bfloat16),
            query_block,
            preferred_element_type=jnp.float32,
        )
        return (key_grad, value_grad)

    grads = (zero_rows, zero_rows)
    grads = key_tile(grads, q_heads, grad_attn, stats, diagonal)

    def relay_queries(back, carry):
        inner, moving = carry
        moving = from_behind((moving[0], moving[1], moving[2]), "seq", -1)
        valid = place + back <= shards - 1
        live = jnp.broadcast_to(valid, (rows, rows))
        inner = key_tile(inner, moving[0], moving[1], moving[2], live)
        return (inner, moving)

    grads, moved = lax.fori_loop(1, shards, relay_queries, (grads, (q_heads, grad_attn, stats)))
    key_grad, value_grad = grads
    grad_q = grad_query.astype(jnp.bfloat16).reshape(rows, heads_here * width)
    grad_k = (key_grad * scale).astype(jnp.bfloat16).reshape(rows, heads_here * width)
    grad_v = value_grad.astype(jnp.bfloat16).reshape(rows, heads_here * width)
    span_taps = filters.shape[1]
    groups = filters.shape[0]
    channels = gate_q.shape[1]
    dz = (grad_y.astype(jnp.float32) * gate_q.astype(jnp.float32)).astype(jnp.bfloat16)
    rim = from_behind(dz[: span_taps - 1], "seq", -1)
    grad_gate = (grad_y.astype(jnp.float32) * conv_out.astype(jnp.float32)).astype(jnp.bfloat16)
    padded = jnp.concatenate([dz, rim], axis=0).astype(jnp.float32)
    taps = jnp.tile(filters.T, (1, channels // groups))
    mixed = feat_k.astype(jnp.float32) * feat_v.astype(jnp.float32)
    numbers = ("NWC", "WIO", "NWC")
    dw = lax.conv_general_dilated(
        padded[None],
        taps[:, None, :],
        (1,),
        "VALID",
        dimension_numbers=numbers,
        feature_group_count=channels,
        precision=lax.Precision.HIGHEST,
    )[0]
    local_terms = lax.conv_general_dilated(
        padded[None],
        mixed[:, None, :],
        (1,),
        "VALID",
        dimension_numbers=numbers,
        feature_group_count=channels,
        precision=lax.Precision.HIGHEST,
    )[0]
    grad_feat_k = (dw * feat_v.astype(jnp.float32)).astype(jnp.bfloat16)
    grad_feat_v = (dw * feat_k.astype(jnp.float32)).astype(jnp.bfloat16)
    local_terms = jnp.sum(local_terms.reshape(span_taps, channels // groups, groups), axis=1).T
    filter_total = lax.psum(local_terms, ("seq", "tp"))
    count_all = rows * shards * channels * lax.axis_size("tp") / groups
    grad_filters = filter_total * (1.0 / count_all**0.5)
    return (grad_q, grad_k, grad_v, grad_gate, grad_feat_k, grad_feat_v, grad_filters)


MESH = pl.DeviceIdType.MESH
LANES = 128
LOG2E = 1.4426950408889634
CHIPS = 4
CROSS = {0: ((1, 2), (1, 1), (2, 2), (2, 1)), 1: ((1, 2), (2, 2)), 2: ((0, 1), (3, 1)), 3: ((0, 2), (0, 1), (3, 2), (3, 1))}
DELTAS = {2: (1,), 3: (2, 1)}


def kernel(
    n,
    tp,
    q_in,
    k_in,
    v_in,
    do_in,
    ao_in,
    gate_in,
    fk_in,
    fv_in,
    gy_in,
    filters,
    gq_out,
    gk_out,
    gv_out,
    gfk_out,
    gfv_out,
    gf_out,
    heads_q,
    heads_k,
    heads_v,
    heads_do,
    keys_t,
    delta_mine,
    delta_all,
    lse_mine,
    lse_in,
    edge_mine,
    edge_in,
    part_mine,
    part_in,
    do_here,
    ao_here,
    gate,
    fk,
    fv,
    gy,
    dz_here,
    dz_rim,
    dz_all,
    rim_all,
    dw_all,
    taps,
    terms,
    partial_mine,
    partial_in,
    across,
    scores,
    grad_t,
    acc_k,
    acc_v,
    res_q,
    res_k,
    res_v,
    load_sem,
    send_x,
    recv_x,
    send_d,
    recv_d,
    send_l,
    recv_l,
    send_e,
    recv_e,
    send_p,
    recv_p,
    send_rim,
    recv_rim,
    send_out,
    recv_out,
    own_out,
    send_rs,
    recv_rs,
    send_tp,
    recv_tp,
    send_ag,
    recv_ag,
):
    me = lax.axis_index("seq")
    lane = lax.axis_index("tp")
    z = lax.div(me, 2)
    core = lax.rem(me, 2)
    other = 1 - core
    partner = 2 * z + other
    rows, width = q_in.shape[0], LANES
    count = q_in.shape[1] // width // 2
    half = count * width
    tile = 2 * rows
    channels = gy_in.shape[1]
    span = filters.shape[1]
    scale = 1.0 / width**0.5

    def chunk(i, size):
        return pl.ds(pl.multiple_of(i * size, size), size)

    def remote(src, dst, send, recv, device):
        return pltpu.make_async_remote_copy(
            src_ref=src,
            dst_ref=dst,
            send_sem=send,
            recv_sem=recv,
            device_id={"seq": device},
            device_id_type=MESH,
        )

    loads = [
        pltpu.make_async_copy(src, dst, load_sem.at[i])
        for i, (src, dst) in enumerate(
            (
                (do_in, do_here),
                (ao_in, ao_here),
                (gy_in, gy),
                (gate_in, gate),
                (fk_in, fk),
                (fv_in, fv),
            )
        )
    ]
    for load in loads:
        load.start()

    barrier = pltpu.get_barrier_semaphore()
    for d in range(1, n):
        pl.semaphore_signal(
            barrier, inc=1, device_id={"seq": lax.rem(me + d, n)}, device_id_type=MESH
        )
    for d in range(1, tp):
        pl.semaphore_signal(
            barrier, inc=1, device_id={"tp": lax.rem(lane + d, tp)}, device_id_type=MESH
        )
    pl.semaphore_wait(barrier, n - 1 + tp - 1)

    ins = (q_in, k_in, v_in, do_in)
    heads = (heads_q, heads_k, heads_v, heads_do)

    def move(a, h, chip, to):
        return remote(
            ins[a].at[:, chunk(to * count + h, width)],
            heads[a].at[h, chunk(me, rows), :],
            send_x.at[a, chip, to],
            recv_x.at[a, z, h],
            2 * chip + to,
        )

    def moved(a, chip, to):
        return remote(
            ins[a].at[:, chunk(to, half)],
            ins[a].at[:, chunk(to, half)],
            send_x.at[a, chip, to],
            recv_x.at[a, chip, 0],
            2 * chip + to,
        )

    def own(a, h):
        return pltpu.make_async_copy(
            ins[a].at[:, chunk(core * count + h, width)],
            heads[a].at[h, chunk(me, rows), :],
            recv_x.at[a, z, h],
        )

    def arrive(a, chip, h):
        at = heads[a].at[h, chunk(chip, tile), :]
        remote(at, at, send_x.at[a, 0, 0], recv_x.at[a, chip, h], partner).wait_recv()

    def exchange(h):
        for a in (0, 1, 3, 2):
            own(a, h).start()
            move(a, h, z, other).start()

    def outward(h):
        for chip in range(CHIPS):

            @pl.when(z == chip)
            def _():
                for a, to in CROSS[chip]:
                    for side in range(2):
                        move(a, h, to, side).start()

    def rim_copy():
        return remote(dz_here, dz_rim, send_rim, recv_rim, lax.rem(me + n - 1, n))

    def delta_copy(chip, to):
        return remote(
            delta_mine.at[to],
            delta_all.at[me],
            send_d.at[chip, to],
            recv_d.at[me],
            2 * chip + to,
        )

    def delta_wait(chip):
        for side in range(2):
            b = 2 * chip + side
            at = delta_all.at[b]

            @pl.when(b != me)
            def _():
                remote(at, at, send_d.at[0, 0], recv_d.at[b], partner).wait_recv()

    for h in range(count):
        exchange(h)
    outward(0)

    loads[0].wait()
    loads[1].wait()
    for h in range(2 * count):
        at = slice(h * width, (h + 1) * width)
        prod = do_here[:, at].astype(jnp.float32) * ao_here[:, at].astype(jnp.float32)
        line = jnp.sum(prod.T, axis=0, keepdims=True)
        delta_mine[h // count, h % count] = jnp.broadcast_to(line, (8, rows))
    delta_all[me] = delta_mine[core]
    delta_copy(z, other).start()
    for chip, targets in DELTAS.items():

        @pl.when(z == chip)
        def _():
            for to in targets:
                for side in range(2):
                    delta_copy(to, side).start()

    loads[2].wait()
    loads[3].wait()
    tiles = channels // LANES
    for t in range(tiles):
        at = slice(t * LANES, (t + 1) * LANES)
        dz = (gy[:, at].astype(jnp.float32) * gate[:, at].astype(jnp.float32)).astype(jnp.bfloat16)
        dz_here[:, at] = dz
        dz_all[t, 0:rows, :] = dz.astype(jnp.float32)
        dz_all[t, rows : rows + 8, :] = jnp.zeros((8, LANES), jnp.float32)
    outward(1)

    @pl.when(me > 0)
    def _():
        rim_copy().start()

    for h in range(2, count):
        outward(h)

    key_id = lax.broadcasted_iota(jnp.int32, (tile, tile), 0)
    query_id = lax.broadcasted_iota(jnp.int32, (tile, tile), 1)
    nt = (((1,), (1,)), ((), ()))
    nn = (((1,), (0,)), ((), ()))

    def dot(a, b, dims):
        return lax.dot_general(a, b, dims, preferred_element_type=jnp.float32)

    def at_tile(i):
        return slice(i * tile, (i + 1) * tile)

    def log_sums(h, i, keys):
        query = heads_q[h, at_tile(i), :]
        top = None
        for j in keys:
            raw = dot(heads_k[h, at_tile(j), :], query, nt)
            if j == i:
                raw = jnp.where(key_id <= query_id, raw, -1e30)
            scores[at_tile(j), :] = raw
            high = jnp.max(raw, axis=0, keepdims=True)
            top = high if top is None else jnp.maximum(top, high)
        total = jnp.zeros_like(top)
        for j in keys:
            weight = jnp.exp2((scores[at_tile(j), :] - top) * (scale * LOG2E))
            total = total + jnp.sum(weight, axis=0, keepdims=True)
        return top * scale + jnp.log(total)

    def wire(x):
        high = x.astype(jnp.bfloat16).astype(jnp.float32)
        return high + (x - high).astype(jnp.bfloat16).astype(jnp.float32)

    def delta_row(h, i):
        return jnp.concatenate(
            [delta_all[2 * i, h][0:1, :], delta_all[2 * i + 1, h][0:1, :]], axis=1
        )

    def turn_keys(h, j):
        keys_t[:, at_tile(j)] = heads_k[h, at_tile(j), :].T

    def pair(h, i, j, lse, want_q, want_k, fresh_q=False, fresh_k=False):
        query = heads_q[h, at_tile(i), :]
        upstream = heads_do[h, at_tile(i), :]
        delta = delta_row(h, i)
        lse_w = wire(lse)
        base = lse if want_q else lse_w
        raw = dot(heads_k[h, at_tile(j), :], query, nt)
        prob = jnp.exp2(raw * (scale * LOG2E) - base * LOG2E)
        if i == j:
            prob = jnp.where(key_id <= query_id, prob, 0.0)
        dprob = dot(heads_v[h, at_tile(j), :], upstream, nt)
        if want_q:
            dscore = prob * (dprob - delta)
            big = dscore.astype(jnp.bfloat16)
            rest = (dscore - big.astype(jnp.float32)).astype(jnp.bfloat16)
            turned = keys_t[:, at_tile(j)]
            grad = dot(turned, big, nn) + dot(turned, rest, nn)
            grad_t[...] = grad if fresh_q else grad_t[...] + grad
        if want_k:
            prob_k = prob * jnp.exp(lse - lse_w) if want_q else prob
            dscore_k = (prob_k * (dprob - wire(delta))).astype(jnp.bfloat16)
            grad_v = dot(prob_k.astype(jnp.bfloat16), upstream, nn)
            grad_k = dot(dscore_k, query, nn)
            acc_v[j % 2] = grad_v if fresh_k else acc_v[j % 2] + grad_v
            acc_k[j % 2] = grad_k if fresh_k else acc_k[j % 2] + grad_k

    results = ((res_q, gq_out), (res_k, gk_out), (res_v, gv_out))

    def give(a, h):
        src, dst = results[a]
        at = chunk(core * count + h, width)
        pltpu.make_async_copy(
            src.at[h, chunk(core, rows), :], dst.at[:, at], own_out.at[a]
        ).start()
        remote(
            src.at[h, chunk(other, rows), :],
            dst.at[:, at],
            send_out.at[a],
            recv_out.at[a],
            partner,
        ).start()

    def lse_copy(h, chip):
        if chip == 1:
            return remote(
                lse_mine.at[h], lse_in.at[h], send_l.at[h, 0], recv_l.at[h], 2 * chip + core
            )
        return remote(
            lse_mine.at[h, 1], lse_in.at[h, 1], send_l.at[h, 1], recv_l.at[h], 2 * chip + core
        )

    def edge_copy(h):
        return remote(
            edge_mine.at[h], edge_in.at[h], send_e.at[h], recv_e.at[h], 2 * 2 + core
        )

    def part_copy(h, chip):
        if chip == 0:
            return remote(
                part_mine.at[h], part_in.at[h], send_p.at[h], recv_p.at[h], 2 * chip + core
            )
        return remote(
            part_mine.at[h, 0], part_in.at[h, 0], send_p.at[h], recv_p.at[h], 2 * chip + core
        )

    def spread(row):
        return jnp.broadcast_to(row, (8, tile))

    def later_sums(h):
        for a, chip in ((0, 2), (1, 2), (1, 0), (1, 1), (0, 3)):
            arrive(a, chip, h)
        edge_copy(h).wait_recv()
        lse_mine[h, 0] = spread(log_sums(h, 2, (0, 1, 2)))
        near = log_sums(h, 3, (0, 1, 2))
        far = edge_in[h][0:1, :]
        top = jnp.maximum(near, far)
        lse_mine[h, 1] = spread(top + jnp.log(jnp.exp(near - top) + jnp.exp(far - top)))
        lse_copy(h, 1).start()
        lse_copy(h, 3).start()

    def head_first(h):
        for a in range(4):
            arrive(a, 0, h)
        turn_keys(h, 0)
        pair(h, 0, 0, log_sums(h, 0, (0,)), True, True, True, True)
        res_q[h] = (grad_t[...] * scale).T.astype(jnp.bfloat16)
        give(0, h)
        part_copy(h, 0).wait_recv()
        res_k[h] = ((acc_k[0] + part_in[h, 0].astype(jnp.float32)) * scale).astype(jnp.bfloat16)
        res_v[h] = (acc_v[0] + part_in[h, 1].astype(jnp.float32)).astype(jnp.bfloat16)
        give(1, h)
        give(2, h)

    def head_second(h):
        for a in range(4):
            arrive(a, 1, h)
        arrive(1, 0, h)
        lse = log_sums(h, 1, (0, 1))
        turn_keys(h, 0)
        turn_keys(h, 1)
        arrive(2, 0, h)
        pair(h, 1, 0, lse, True, True, True, True)
        pair(h, 1, 1, lse, True, True, False, True)
        res_q[h] = (grad_t[...] * scale).T.astype(jnp.bfloat16)
        give(0, h)
        lse_copy(h, 1).wait_recv()
        for i in (2, 3):
            arrive(0, i, h)
            arrive(3, i, h)
            for j in (0, 1):
                pair(h, i, j, lse_in[h, i - 2][0:1, :], False, True)
        part_mine[h, 0] = acc_k[0].astype(jnp.bfloat16)
        part_mine[h, 1] = acc_v[0].astype(jnp.bfloat16)
        part_copy(h, 0).start()
        res_k[h] = (acc_k[1] * scale).astype(jnp.bfloat16)
        res_v[h] = acc_v[1].astype(jnp.bfloat16)
        give(1, h)
        give(2, h)

    def head_third(h):
        @pl.when(h < count - 1)
        def _():
            later_sums(h + 1)

        for j in range(3):
            turn_keys(h, j)
        for a, chip in ((2, 2), (3, 2), (2, 0), (2, 1), (3, 3)):
            arrive(a, chip, h)
        lse = lse_mine[h, 1][0:1, :]
        pair(h, 3, 0, lse, True, False, True)
        pair(h, 3, 1, lse, True, False)
        pair(h, 3, 2, lse, True, True, False, True)
        part_mine[h, 0] = grad_t[...].T.astype(jnp.bfloat16)
        part_copy(h, 3).start()
        lse = lse_mine[h, 0][0:1, :]
        pair(h, 2, 0, lse, True, False, True)
        pair(h, 2, 1, lse, True, False)
        pair(h, 2, 2, lse, True, True)
        res_q[h] = (grad_t[...] * scale).T.astype(jnp.bfloat16)
        res_k[h] = (acc_k[0] * scale).astype(jnp.bfloat16)
        res_v[h] = acc_v[0].astype(jnp.bfloat16)
        for a in range(3):
            give(a, h)

    def head_last(h):
        for a in (2, 3):
            arrive(a, 3, h)
        lse_copy(h, 3).wait_recv()
        turn_keys(h, 3)
        pair(h, 3, 3, lse_in[h, 1][0:1, :], True, True, True, True)
        res_k[h] = (acc_k[1] * scale).astype(jnp.bfloat16)
        res_v[h] = acc_v[1].astype(jnp.bfloat16)
        give(1, h)
        give(2, h)
        part_copy(h, 3).wait_recv()
        total = grad_t[...].T + part_in[h, 0].astype(jnp.float32)
        res_q[h] = (total * scale).astype(jnp.bfloat16)
        give(0, h)

    for chip in range(CHIPS):

        @pl.when(z == chip)
        def _():
            delta_wait(chip)

    @pl.when(z == 3)
    def _():
        def edge(h, carry):
            arrive(0, 3, h)
            arrive(1, 3, h)
            edge_mine[h] = spread(log_sums(h, 3, (3,)))
            edge_copy(h).start()
            return carry

        lax.fori_loop(0, count, edge, 0)

    loads[4].wait()
    loads[5].wait()
    terms[...] = jnp.zeros_like(terms)
    both = jnp.concatenate([filters[...]] * (LANES // filters.shape[0]), axis=0)
    taps[...] = both.T

    def conv_own(t, carry):
        at = pl.ds(pl.multiple_of(t * LANES, LANES), LANES)
        mixed = fk[:, at].astype(jnp.float32) * fv[:, at].astype(jnp.float32)
        for a in range(span // 8):
            size = rows - 8 * a
            part = None
            for b in range(8):
                tap = 8 * a + b
                x = dz_all[t, tap : tap + size, :]
                term = x * taps[tap : tap + 1, :]
                part = term if part is None else part + term
                prod = (x * mixed[0:size]).reshape(size // 8, 8, LANES)
                terms[tap] = terms[tap] + jnp.sum(prod, axis=0)
            if a == 0:
                dw_all[t] = part
            else:
                dw_all[t, 0:size, :] = dw_all[t, 0:size, :] + part
        return carry

    lax.fori_loop(0, tiles, conv_own, 0)

    @pl.when(z == 1)
    def _():
        delta_wait(2)
        delta_wait(3)

    @pl.when(z == 2)
    def _():
        delta_wait(3)
        later_sums(0)

    def rim_part():
        @pl.when(me < n - 1)
        def _():
            rim_copy().wait_recv()
            for t in range(tiles):
                at = slice(t * LANES, (t + 1) * LANES)
                rim_all[t, 0:8, :] = jnp.zeros((8, LANES), jnp.float32)
                rim_all[t, 8 : rows + 8, :] = dz_rim[:, at].astype(jnp.float32)

        @pl.when(me == n - 1)
        def _():
            for t in range(tiles):
                rim_all[t, 0 : rows + 8, :] = jnp.zeros((rows + 8, LANES), jnp.float32)

        def conv_rim(t, carry):
            at = pl.ds(pl.multiple_of(t * LANES, LANES), LANES)
            left = fk[:, at].astype(jnp.float32)
            right = fv[:, at].astype(jnp.float32)
            mixed = left * right
            for a in range(span // 8):
                size = 8 * (a + 1)
                part = None
                for b in range(8):
                    tap = 8 * a + b
                    x = rim_all[t, b : b + size, :]
                    term = x * taps[tap : tap + 1, :]
                    part = term if part is None else part + term
                    prod = (x * mixed[rows - size : rows]).reshape(size // 8, 8, LANES)
                    terms[tap] = terms[tap] + jnp.sum(prod, axis=0)
                dw_all[t, rows - size : rows, :] = dw_all[t, rows - size : rows, :] + part
            acc = dw_all[t]
            gfk_out[:, at] = (acc * right).astype(jnp.bfloat16)
            gfv_out[:, at] = (acc * left).astype(jnp.bfloat16)
            return carry

        lax.fori_loop(0, tiles, conv_rim, 0)
    share = gf_out.shape[0] // n

    def slab(i):
        return chunk(i, share)

    def seq_copy(d):
        peer = lax.rem(me + d, n)
        return remote(
            partial_mine.at[slab(peer), :], partial_in.at[me], send_rs.at[d], recv_rs.at[d], peer
        )

    def tp_copy(d):
        return pltpu.make_async_remote_copy(
            src_ref=across.at[lane],
            dst_ref=across.at[lane],
            send_sem=send_tp.at[d],
            recv_sem=recv_tp.at[d],
            device_id={"tp": lax.rem(lane + d, tp)},
            device_id_type=MESH,
        )

    def all_copy(d):
        at = gf_out.at[slab(me), :]
        return remote(at, at, send_ag.at[d], recv_ag.at[d], lax.rem(me + d, n))

    def sum_here():
        per_lane = jnp.sum(terms[...], axis=1)
        groups = gf_out.shape[0]
        folded = per_lane
        for g in range(1, LANES // groups):
            folded = folded + pltpu.roll(per_lane, g * groups, 1)
        partial_mine[...] = folded.T[0:groups, :]
        partial_in[me] = partial_mine[slab(me), :]
        for d in range(1, n):
            seq_copy(d).start()

    def sum_seq():
        for d in range(1, n):
            seq_copy(d).wait_recv()
        total = partial_in[0]
        for i in range(1, n):
            total = total + partial_in[i]
        across[lane] = total
        for d in range(1, tp):
            tp_copy(d).start()

    def sum_tp():
        for d in range(1, tp):
            tp_copy(d).wait_recv()
        total = across[0]
        for i in range(1, tp):
            total = total + across[i]
        count_all = rows * n * channels * tp / gf_out.shape[0]
        gf_out[slab(me), :] = total * (1.0 / count_all**0.5)
        for d in range(1, n):
            all_copy(d).start()

    def per_head(h, carry):
        @pl.when(h == count // 2)
        def _():
            rim_part()
            sum_here()

        @pl.when(h == count - 1)
        def _():
            sum_seq()

        for chip, work in enumerate((head_first, head_second, head_third, head_last)):

            @pl.when(z == chip)
            def _():
                work(h)

        return carry

    lax.fori_loop(0, count, per_head, 0)
    sum_tp()

    @pl.when(me > 0)
    def _():
        rim_copy().wait_send()

    for a in range(4):
        moved(a, z, other).wait_send()
    delta_copy(z, other).wait_send()
    for chip in range(CHIPS):

        @pl.when(z == chip)
        def _():
            for a, to in CROSS[chip]:
                for side in range(2):
                    moved(a, to, side).wait_send()
            for to in DELTAS.get(chip, ()):
                for side in range(2):
                    delta_copy(to, side).wait_send()
            for h in range(count):
                if chip == 1:
                    part_copy(h, 0).wait_send()
                if chip == 2:
                    part_copy(h, 3).wait_send()
                    lse_copy(h, 1).wait_send()
                    lse_copy(h, 3).wait_send()
                if chip == 3:
                    edge_copy(h).wait_send()

    for a in range(3):
        dst = results[a][1]
        mine = dst.at[:, chunk(core, half)]
        theirs = dst.at[:, chunk(other, half)]
        pltpu.make_async_copy(mine, mine, own_out.at[a]).wait()
        remote(theirs, theirs, send_out.at[a], recv_out.at[a], partner).wait()
    for d in range(1, n):
        seq_copy(d).wait_send()
        all_copy(d).wait()
    for d in range(1, tp):
        tp_copy(d).wait_send()


def finish(
    gy_in,
    co_in,
    gq_in,
    gk_in,
    gv_in,
    gfk_in,
    gfv_in,
    gf_in,
    gq_out,
    gk_out,
    gv_out,
    gg_out,
    gfk_out,
    gfv_out,
    gf_out,
    gy,
    co,
    gg,
    gq,
    gk,
    gv,
    gfk,
    gfv,
    gf,
    sem_in,
    sem_out,
):
    sources = (gy_in, co_in, gq_in, gk_in, gv_in, gfk_in, gfv_in, gf_in)
    holds = (gy, co, gq, gk, gv, gfk, gfv, gf)
    taken = [
        pltpu.make_async_copy(src, dst, sem_in.at[i])
        for i, (src, dst) in enumerate(zip(sources, holds))
    ]
    for copy in taken:
        copy.start()
    given = []

    def give(src, dst):
        copy = pltpu.make_async_copy(src, dst, sem_out.at[len(given)])
        copy.start()
        given.append(copy)

    outs = (gq_out, gk_out, gv_out, gfk_out, gfv_out, gf_out)
    taken[0].wait()
    taken[1].wait()
    gg[...] = (gy[...].astype(jnp.float32) * co[...].astype(jnp.float32)).astype(jnp.bfloat16)
    give(gg, gg_out)
    for i, dst in enumerate(outs):
        taken[2 + i].wait()
        give(holds[2 + i], dst)
    for copy in given:
        copy.wait()


def local_heads(
    n,
    tp,
    q_heads,
    k_heads,
    v_heads,
    grad_attn,
    attn_out,
    gate_q,
    feat_k,
    feat_v,
    conv_out,
    grad_y,
    filters,
):
    rows, wide = q_heads.shape
    width = LANES
    count = wide // width // 2
    tile = 2 * rows
    channels = gate_q.shape[1]
    groups, span = filters.shape
    share = groups // n
    tiles = channels // LANES
    bf16, f32 = (jnp.bfloat16, jnp.float32)
    anywhere = pl.BlockSpec(memory_space=pl.ANY)
    inside = pl.BlockSpec(memory_space=pltpu.VMEM)
    dma = pltpu.SemaphoreType.DMA
    vmem = pltpu.VMEM
    small = [jax.ShapeDtypeStruct((rows, wide), bf16)] * 3
    large = [jax.ShapeDtypeStruct((rows, channels), bf16)] * 2
    last = [jax.ShapeDtypeStruct((groups, span), f32)]
    parts = pl.pallas_call(
        functools.partial(kernel, n, tp),
        out_shape=small + large + last,
        in_specs=[anywhere] * 9 + [inside],
        out_specs=[anywhere] * 3 + [inside] * 3,
        scratch_shapes=(
            [vmem((count, n * rows, width), bf16)] * 4
            + [
                vmem((width, n * rows), bf16),
                vmem((2, count, 8, rows), f32),
                vmem((n, count, 8, rows), f32),
                vmem((count, 2, 8, tile), f32),
                vmem((count, 2, 8, tile), f32),
                vmem((count, 8, tile), f32),
                vmem((count, 8, tile), f32),
                vmem((count, 2, tile, width), bf16),
                vmem((count, 2, tile, width), bf16),
            ]
            + [vmem((rows, wide), bf16)] * 2
            + [vmem((rows, channels), bf16)] * 6
            + [
                vmem((tiles, rows + 8, LANES), f32),
                vmem((tiles, rows + 16, LANES), f32),
                vmem((tiles, rows, LANES), f32),
                vmem((span, LANES), f32),
                vmem((span, 8, LANES), f32),
                vmem((groups, span), f32),
                vmem((n, share, span), f32),
                vmem((tp, share, span), f32),
                vmem((n * rows, tile), f32),
                vmem((width, tile), f32),
            ]
            + [vmem((2, tile, width), f32)] * 2
            + [vmem((count, tile, width), bf16)] * 3
            + [
                dma((6,)),
                dma((4, CHIPS, 2)),
                dma((4, CHIPS, count)),
                dma((CHIPS, 2)),
                dma((n,)),
                dma((count, 2)),
                dma((count,)),
                dma((count,)),
                dma((count,)),
                dma((count,)),
                dma((count,)),
                dma,
                dma,
                dma((3,)),
                dma((3,)),
                dma((3,)),
                dma((n,)),
                dma((n,)),
                dma((tp,)),
                dma((tp,)),
                dma((n,)),
                dma((n,)),
            ]
        ),
        compiler_params=pltpu.CompilerParams(
            collective_id=0, has_side_effects=True, vmem_limit_bytes=67043328
        ),
    )(q_heads, k_heads, v_heads, grad_attn, attn_out, gate_q, feat_k, feat_v, grad_y, filters)
    return pl.pallas_call(
        finish,
        out_shape=small + large[:1] + large + last,
        in_specs=[anywhere] * 8,
        out_specs=[anywhere] * 7,
        scratch_shapes=(
            [vmem((rows, channels), bf16)] * 3
            + [vmem((rows, wide), bf16)] * 3
            + [vmem((rows, channels), bf16)] * 2
            + [vmem((groups, span), f32), dma((8,)), dma((7,))]
        ),
    )(grad_y, conv_out, *parts)


def local(*args):
    n, tp = (lax.axis_size("seq"), lax.axis_size("tp"))
    rows, wide = args[0].shape
    groups, span = args[10].shape
    fits = (
        HEADS // tp == n
        and n == 2 * CHIPS
        and tp > 1
        and rows == LANES
        and wide == n * LANES
        and span <= rows
        and span == LANES
        and LANES % groups == 0
        and groups % (8 * n) == 0
    )
    if fits:
        return tuple(local_heads(n, tp, *args))
    return local_ring(*args)


def solution(mesh):
    in_specs = (
        P("seq", "tp"),
        P("seq", "tp"),
        P("seq", "tp"),
        P("seq", "tp"),
        P("seq", "tp"),
        P("seq", "tp"),
        P("seq", "tp"),
        P("seq", "tp"),
        P("seq", "tp"),
        P("seq", "tp"),
        P(),
    )
    out_specs = (
        P("seq", "tp"),
        P("seq", "tp"),
        P("seq", "tp"),
        P("seq", "tp"),
        P("seq", "tp"),
        P("seq", "tp"),
        P(),
    )
    return jax.shard_map(local, mesh=mesh, in_specs=in_specs, out_specs=out_specs, check_vma=False)
```

time: 75.8 us -> 79.5 us (1.049)
  Pallas kernels: 67.8 us -> 78.7 us
  local copies, waits for them, and re-layouts: 7.01 us -> 0 us
    pallas_call x1 -> x2, Pallas kernels: 67.8 us -> 78.7 us  [the longest x1 75.8 us: local_heads(): pl.pallas_call(functools.partial(kernel, n, tp), out_shape=small + large...]
    unnamed x19 -> x0, local copies, waits for them, and re-layouts: 7.01 us -> none
where the time goes in v1:
time: 79.5 us; the launch traced here: 79.3 us
  Pallas kernels  78.7 us (99%)
    pallas_call x1, Pallas kernels, local_heads(): pl.pallas_call(functools.partial(kernel, n, tp), out_shape=small + large...  75.8 us
    pallas_call x1, Pallas kernels, local_heads(): pl.pallas_call(finish, out_shape=small + large[:1] + large + last, in_spe...  2.85 us

profile of v1, /device:TPU:0, one launch (start us, length us, event | category | flops | bytes accessed | tf_op | source)
XLA Modules:
  0.0 79.3 jit_solution(2725477851613001120)
XLA Ops:
  0.6 75.8 %shard_map.162 = (bf16[128,1024]{1,0:T(8,128)(2,1)}, bf16[128,1024]{1,0:T(8,128)(2,1)}, bf16[128,1024]{1,0:T(8,128)(2,1)}, bf16[128,2048]{1,0:T(8,128)(2,1)}, bf...) custom-call(bf16[128,1024]{1,0:T(8,128)(2,1)} %q_in.1, bf16[128,1024]{1,0:T(8,128)(2,1)} %k_in.1, bf16[128,1024]{1,0:T(8,128)(2,1)} %v_in.1, ...), custom_call_target="tpu_custom_call" | custom-call | tf_op jit(solution)/shard_map/pallas_call | solution.py:925
  76.4 2.9 %shard_map.163 = (bf16[128,1024]{1,0:T(8,128)(2,1)}, bf16[128,1024]{1,0:T(8,128)(2,1)}, bf16[128,1024]{1,0:T(8,128)(2,1)}, bf16[128,2048]{1,0:T(8,128)(2,1)}, bf...) custom-call(bf16[128,2048]{1,0:T(8,128)(2,1)} %gy_in.3, bf16[128,2048]{1,0:T(8,128)(2,1)} %co_in.1, ...), custom_call_target="tpu_custom_call" | custom-call | tf_op jit(solution)/shard_map/pallas_call | solution.py:988

commit v2 on v1

--- a/solution.py
+++ b/solution.py
@@ -412,24 +412,6 @@
                 for side in range(2):
                     delta_copy(to, side).start()
 
-    loads[2].wait()
-    loads[3].wait()
-    tiles = channels // LANES
-    for t in range(tiles):
-        at = slice(t * LANES, (t + 1) * LANES)
-        dz = (gy[:, at].astype(jnp.float32) * gate[:, at].astype(jnp.float32)).astype(jnp.bfloat16)
-        dz_here[:, at] = dz
-        dz_all[t, 0:rows, :] = dz.astype(jnp.float32)
-        dz_all[t, rows : rows + 8, :] = jnp.zeros((8, LANES), jnp.float32)
-    outward(1)
-
-    @pl.when(me > 0)
-    def _():
-        rim_copy().start()
-
-    for h in range(2, count):
-        outward(h)
-
     key_id = lax.broadcasted_iota(jnp.int32, (tile, tile), 0)
     query_id = lax.broadcasted_iota(jnp.int32, (tile, tile), 1)
     nt = (((1,), (1,)), ((), ()))
@@ -549,6 +531,10 @@
         lse_copy(h, 1).start()
         lse_copy(h, 3).start()
 
+        @pl.when(h < count - 2)
+        def _():
+            outward(h + 2)
+
     def head_first(h):
         for a in range(4):
             arrive(a, 0, h)
@@ -628,12 +614,6 @@
         res_q[h] = (total * scale).astype(jnp.bfloat16)
         give(0, h)
 
-    for chip in range(CHIPS):
-
-        @pl.when(z == chip)
-        def _():
-            delta_wait(chip)
-
     @pl.when(z == 3)
     def _():
         def edge(h, carry):
@@ -644,6 +624,36 @@
             return carry
 
         lax.fori_loop(0, count, edge, 0)
+
+    loads[2].wait()
+    loads[3].wait()
+    tiles = channels // LANES
+    for t in range(tiles):
+        at = slice(t * LANES, (t + 1) * LANES)
+        dz = (gy[:, at].astype(jnp.float32) * gate[:, at].astype(jnp.float32)).astype(jnp.bfloat16)
+        dz_here[:, at] = dz
+        dz_all[t, 0:rows, :] = dz.astype(jnp.float32)
+        dz_all[t, rows : rows + 8, :] = jnp.zeros((8, LANES), jnp.float32)
+
+    @pl.when(me > 0)
+    def _():
+        rim_copy().start()
+
+    outward(1)
+
+    @pl.when(z != 2)
+    def _():
+        outward(2)
+
+    @pl.when(z < 2)
+    def _():
+        outward(count - 1)
+
+    for chip in range(CHIPS):
+
+        @pl.when(z == chip)
+        def _():
+            delta_wait(chip)
 
     loads[4].wait()
     loads[5].wait()
@@ -776,10 +786,14 @@
             all_copy(d).start()
 
     def per_head(h, carry):
-        @pl.when(h == count // 2)
+        @pl.when(h == z * (CHIPS - 1 - z))
         def _():
             rim_part()
             sum_here()
+
+            @pl.when(z == 3)
+            def _():
+                outward(count - 1)
 
         @pl.when(h == count - 1)
         def _():

time: 79.5 us -> 65.9 us (0.83)
  Pallas kernels: 78.7 us -> 65 us
    pallas_call x1, Pallas kernels: 75.8 us -> 62.1 us  [local_heads(): pl.pallas_call(functools.partial(kernel, n, tp), out_shape=small + large...]
where the time goes in v2:
time: 65.9 us; the launch traced here: 65.6 us
  Pallas kernels  65 us (99%)
    pallas_call x1, Pallas kernels, local_heads(): pl.pallas_call(functools.partial(kernel, n, tp), out_shape=small + large...  62.1 us
    pallas_call x1, Pallas kernels, local_heads(): pl.pallas_call(finish, out_shape=small + large[:1] + large + last, in_spe...  2.85 us

profile of v2, /device:TPU:0, one launch (start us, length us, event | category | flops | bytes accessed | tf_op | source)
XLA Modules:
  0.0 65.6 jit_solution(17384101152545164961)
XLA Ops:
  0.6 62.1 %shard_map.162 = (bf16[128,1024]{1,0:T(8,128)(2,1)}, bf16[128,1024]{1,0:T(8,128)(2,1)}, bf16[128,1024]{1,0:T(8,128)(2,1)}, bf16[128,2048]{1,0:T(8,128)(2,1)}, bf...) custom-call(bf16[128,1024]{1,0:T(8,128)(2,1)} %q_in.1, bf16[128,1024]{1,0:T(8,128)(2,1)} %k_in.1, bf16[128,1024]{1,0:T(8,128)(2,1)} %v_in.1, ...), custom_call_target="tpu_custom_call" | custom-call | tf_op jit(solution)/shard_map/pallas_call | solution.py:939
  62.8 2.9 %shard_map.163 = (bf16[128,1024]{1,0:T(8,128)(2,1)}, bf16[128,1024]{1,0:T(8,128)(2,1)}, bf16[128,1024]{1,0:T(8,128)(2,1)}, bf16[128,2048]{1,0:T(8,128)(2,1)}, bf...) custom-call(bf16[128,2048]{1,0:T(8,128)(2,1)} %gy_in.3, bf16[128,2048]{1,0:T(8,128)(2,1)} %co_in.1, ...), custom_call_target="tpu_custom_call" | custom-call | tf_op jit(solution)/shard_map/pallas_call | solution.py:1002

commit v3 on v2

--- a/solution.py
+++ b/solution.py
@@ -564,21 +564,19 @@
         for i in (2, 3):
             arrive(0, i, h)
             arrive(3, i, h)
-            for j in (0, 1):
-                pair(h, i, j, lse_in[h, i - 2][0:1, :], False, True)
-        part_mine[h, 0] = acc_k[0].astype(jnp.bfloat16)
-        part_mine[h, 1] = acc_v[0].astype(jnp.bfloat16)
-        part_copy(h, 0).start()
+            pair(h, i, 0, lse_in[h, i - 2][0:1, :], False, True)
+            if i == 3:
+                part_mine[h, 0] = acc_k[0].astype(jnp.bfloat16)
+                part_mine[h, 1] = acc_v[0].astype(jnp.bfloat16)
+                part_copy(h, 0).start()
+            pair(h, i, 1, lse_in[h, i - 2][0:1, :], False, True)
         res_k[h] = (acc_k[1] * scale).astype(jnp.bfloat16)
         res_v[h] = acc_v[1].astype(jnp.bfloat16)
         give(1, h)
         give(2, h)
 
     def head_third(h):
-        @pl.when(h < count - 1)
-        def _():
-            later_sums(h + 1)
-
+        later_sums(h)
         for j in range(3):
             turn_keys(h, j)
         for a, chip in ((2, 2), (3, 2), (2, 0), (2, 1), (3, 3)):
@@ -690,7 +688,6 @@
     @pl.when(z == 2)
     def _():
         delta_wait(3)
-        later_sums(0)
 
     def rim_part():
         @pl.when(me < n - 1)
@@ -786,7 +783,7 @@
             all_copy(d).start()
 
     def per_head(h, carry):
-        @pl.when(h == z * (CHIPS - 1 - z))
+        @pl.when(h == 0)
         def _():
             rim_part()
             sum_here()
@@ -795,9 +792,13 @@
             def _():
                 outward(count - 1)
 
+        @pl.when(h == count - 2)
+        def _():
+            sum_seq()
+
         @pl.when(h == count - 1)
         def _():
-            sum_seq()
+            sum_tp()
 
         for chip, work in enumerate((head_first, head_second, head_third, head_last)):
 
@@ -808,7 +809,6 @@
         return carry
 
     lax.fori_loop(0, count, per_head, 0)
-    sum_tp()
 
     @pl.when(me > 0)
     def _():

time: 65.9 us -> 61.9 us (0.939)
  Pallas kernels: 65 us -> 61 us
    pallas_call x1, Pallas kernels: 62.1 us -> 58.1 us  [local_heads(): pl.pallas_call(functools.partial(kernel, n, tp), out_shape=small + large...]
where the time goes in v3:
time: 61.9 us; the launch traced here: 61.6 us
  Pallas kernels  61 us (99%)
  between operations  0.64 us (1%)
    pallas_call x1, Pallas kernels, local_heads(): pl.pallas_call(functools.partial(kernel, n, tp), out_shape=small + large...  58.1 us
    pallas_call x1, Pallas kernels, local_heads(): pl.pallas_call(finish, out_shape=small + large[:1] + large + last, in_spe...  2.85 us

profile of v3, /device:TPU:0, one launch (start us, length us, event | category | flops | bytes accessed | tf_op | source)
XLA Modules:
  0.0 61.6 jit_solution(4736117914971047739)
XLA Ops:
  0.6 58.1 %shard_map.162 = (bf16[128,1024]{1,0:T(8,128)(2,1)}, bf16[128,1024]{1,0:T(8,128)(2,1)}, bf16[128,1024]{1,0:T(8,128)(2,1)}, bf16[128,2048]{1,0:T(8,128)(2,1)}, bf...) custom-call(bf16[128,1024]{1,0:T(8,128)(2,1)} %q_in.1, bf16[128,1024]{1,0:T(8,128)(2,1)} %k_in.1, bf16[128,1024]{1,0:T(8,128)(2,1)} %v_in.1, ...), custom_call_target="tpu_custom_call" | custom-call | tf_op jit(solution)/shard_map/pallas_call | solution.py:939
  58.8 2.9 %shard_map.163 = (bf16[128,1024]{1,0:T(8,128)(2,1)}, bf16[128,1024]{1,0:T(8,128)(2,1)}, bf16[128,1024]{1,0:T(8,128)(2,1)}, bf16[128,2048]{1,0:T(8,128)(2,1)}, bf...) custom-call(bf16[128,2048]{1,0:T(8,128)(2,1)} %gy_in.3, bf16[128,2048]{1,0:T(8,128)(2,1)} %co_in.1, ...), custom_call_target="tpu_custom_call" | custom-call | tf_op jit(solution)/shard_map/pallas_call | solution.py:1002
